TPU v7x, 128 devices: a whole 4x4x4 slice. The times are simulated.
128 devices in a mesh: batch: 4 (over x_lo, core), tiles: 32 (over x_hi, z, y).
Axes of the slice: x: 4 (x_hi: 2, x_lo: 2; x = x_hi * 2 + x_lo), y: 4, z: 4, core: 2. Of those that a mesh axis runs over, the one named last changes fastest.
Arguments:
- hidden: bfloat16 [4, 16384, 3072], P('batch', 'tiles'), may hold values from -6 to 6
- frozen_queries: bfloat16 [4, 16384, 1536], P('batch', 'tiles'), may hold values from -108 to 108
- frozen_keys: bfloat16 [4, 16384, 1536], P('batch', 'tiles'), may hold values from -6.09 to 6.09
- frozen_values: bfloat16 [4, 16384, 1536], P('batch', 'tiles'), may hold values from -6 to 6
- reward_output_gradient: bfloat16 [4, 16384, 1536], P('batch', 'tiles'), may hold values from -6 to 6
- truncation_step: int32 [4], P('batch'), may hold values from 0 to 49
- modulation: float32 [50, 2, 3072], replicated, may hold values from -3 to 3
- adapter_down_weight: bfloat16 [3, 3072, 32], replicated, may hold values from -0.109375 to 0.109375
- adapter_up_weight: bfloat16 [3, 32, 1536], replicated, may hold values from -1 to 1
- window: int32 [128, 27], P('tiles'), may hold values from 0 to 1, as said below
Outputs:
- attended: bfloat16 [4, 16384, 1536], P('batch', 'tiles')
- grad_down: float32 [3, 3072, 32], replicated
- grad_up: float32 [3, 32, 1536], replicated
Inputs may be any that keep to these rules, and one draw needn't show every extreme that they name: `window`: entry 13, the tile itself, is 1 for every tile.
All inputs are finite; a program needn't handle non-finite values.
Results may differ from a plain program's by a relative error of at most 0.012.
The roundings to bfloat16 on the way count: a program that leaves them out, or rounds other values in their place, can miss the bound.
Values may be sent and summed in bfloat16 or wider, within the bound.
No kernel may reach another device: no remote copies, remote signals or barrier semaphores. Data moves between devices by JAX's collectives and lax.ppermute only.
A program may use at most 192 MiB of HBM per device.

v0:
```python
import math
import jax
import jax.numpy as jnp
from jax import lax
from jax.sharding import PartitionSpec as P

HEAD = 128
TILE = 128
GF = 2
GR = 2
precise_variant = lax.Precision.HIGHEST


def extended(x, sides, width):
    for axis, dim in sides:
        peers, length = (lax.axis_size(axis), x.shape[dim])
        up = [(i, (i + 1) % peers) for i in range(peers - 1)]
        down = [(j, i) for i, j in up]
        last = lax.slice_in_dim(x, length - width, length, axis=dim)
        initial = lax.slice_in_dim(x, 0, width, axis=dim)
        before = lax.ppermute(last, axis, up)
        after = lax.ppermute(initial, axis, down)
        x = jnp.concatenate([before, x, after], axis=dim)
    return x


def shifted(value, axis, steps):
    count = lax.axis_size(axis)
    initial, last = (max(0, -steps), min(count, count - steps))
    return lax.ppermute(value, axis, [(source, source + steps) for source in range(initial, last)])


def allowed_keys(window_rows, slab_index, slab_count):
    per_slab = GF * GR
    query_tile = jnp.arange(per_slab, dtype=jnp.int32)
    key_tile = jnp.arange(3 * per_slab, dtype=jnp.int32)
    key_side = key_tile // per_slab
    key_local = key_tile % per_slab
    frame_step = key_local[None, :] // GR - query_tile[:, None] // GR
    row_step = key_local[None, :] % GR - query_tile[:, None] % GR
    offset_code = (key_side[None, :] * 3 + frame_step + 1) * 3 + row_step + 1
    nearby = (jnp.abs(frame_step) <= 1) & (jnp.abs(row_step) <= 1)
    neighbour = slab_index + key_side - 1
    inside = (neighbour >= 0) & (neighbour < slab_count)
    offsets = jnp.arange(27, dtype=jnp.int32)
    listed = jnp.sum(
        jnp.where(offset_code[:, :, None] == offsets[None, None, :], window_rows[:, None, :], 0),
        axis=2,
    )
    tile_mask = nearby & inside[None, :] & (listed > 0)
    return jnp.repeat(jnp.repeat(tile_mask, TILE, axis=0), TILE, axis=1)


def attend_group(pieces, allowed):
    queries, key_rows, value_rows, out_grad = pieces
    scale_root = 1.0 / math.sqrt(HEAD)
    scores = (
        jnp.einsum("qhe,khe->hqk", queries, key_rows, preferred_element_type=jnp.float32)
        * scale_root
    )
    scores = jnp.where(allowed[None], scores, -1e30)
    row_max = jnp.max(scores, axis=2, keepdims=True)
    weights = jnp.where(allowed[None], jnp.exp(scores - row_max), 0.0)
    totals = jnp.sum(weights, axis=2, keepdims=True)
    probs = weights / totals
    probs_low = probs.astype(jnp.bfloat16)
    attended = jnp.einsum("hqk,khe->qhe", probs_low, value_rows, preferred_element_type=jnp.float32)
    prob_grad = jnp.einsum("qhe,khe->hqk", out_grad, value_rows, preferred_element_type=jnp.float32)
    centre = jnp.sum(probs * prob_grad, axis=2, keepdims=True)
    score_grad = (probs * (prob_grad - centre) * scale_root).astype(jnp.bfloat16)
    query_grad = jnp.einsum(
        "hqk,khe->qhe", score_grad, key_rows, preferred_element_type=jnp.float32
    )
    key_grad = jnp.einsum("hqk,qhe->khe", score_grad, queries, preferred_element_type=jnp.float32)
    value_grad = jnp.einsum("hqk,qhe->khe", probs_low, out_grad, preferred_element_type=jnp.float32)
    return (attended, query_grad, key_grad, value_grad)


def attend_all(queries, key_rows, value_rows, out_grad, allowed):
    across = queries.shape[1]
    groups = across // (4 * HEAD)

    def split_heads(tensor):
        return tensor.reshape(tensor.shape[0], groups, 4, HEAD).transpose(1, 0, 2, 3)

    def join_heads(tensor):
        return tensor.transpose(1, 0, 2, 3).reshape(tensor.shape[1], across)

    results = lax.map(
        lambda pieces: attend_group(pieces, allowed),
        (
            split_heads(queries),
            split_heads(key_rows),
            split_heads(value_rows),
            split_heads(out_grad),
        ),
    )
    return tuple((join_heads(result_part) for result_part in results))


def per_device(
    hidden,
    frozen_queries,
    frozen_keys,
    frozen_values,
    reward_output_gradient,
    truncation_step,
    modulation,
    adapter_down_weight,
    adapter_up_weight,
    window,
):
    slab_rows = hidden.shape[1]
    across = frozen_queries.shape[2]
    x_full = hidden[0].astype(jnp.float32)
    row_mean = jnp.mean(x_full, axis=1, keepdims=True)
    centred = x_full - row_mean
    variance = jnp.mean(centred * centred, axis=1, keepdims=True)
    normed = centred * lax.rsqrt(variance + 1e-06)
    picker = (
        lax.broadcasted_iota(jnp.int32, (modulation.shape[0],), 0) == truncation_step[0]
    ).astype(jnp.float32)
    shift_scale = jnp.einsum("s,sjd->jd", picker, modulation, precision=precise_variant)
    input_modulated = normed * (1.0 + shift_scale[1][None, :]) + shift_scale[0][None, :]
    reduced_rank_input = jnp.einsum(
        "mx,pxo->pmo",
        input_modulated.astype(jnp.bfloat16),
        adapter_down_weight,
        preferred_element_type=jnp.float32,
    ).astype(jnp.bfloat16)
    projected_output = jnp.einsum(
        "bfe,beg->bfg", reduced_rank_input, adapter_up_weight, preferred_element_type=jnp.float32
    )
    queries = (frozen_queries[0] + projected_output[0]).astype(jnp.bfloat16)
    key_rows = (frozen_keys[0] + projected_output[1]).astype(jnp.bfloat16)
    value_rows = (frozen_values[0] + projected_output[2]).astype(jnp.bfloat16)
    slab_index = lax.axis_index("tiles")
    allowed = allowed_keys(window, slab_index, lax.axis_size("tiles"))
    expanded_up_weight = adapter_up_weight.astype(jnp.float32)
    low_full = reduced_rank_input.astype(jnp.float32)
    paired = jnp.stack([key_rows, value_rows])[:, None]
    framed = extended(paired, (("tiles", 1),), 1)
    attended, query_grad, key_grad, value_grad = attend_all(
        queries,
        framed[0].reshape(3 * slab_rows, across),
        framed[1].reshape(3 * slab_rows, across),
        reward_output_gradient[0],
        allowed,
    )
    returned = jnp.stack(
        [key_grad.reshape(3, slab_rows, across), value_grad.reshape(3, slab_rows, across)]
    )
    from_above = shifted(returned[:, 0].astype(jnp.bfloat16), "tiles", -1).astype(jnp.float32)
    from_below = shifted(returned[:, 2].astype(jnp.bfloat16), "tiles", 1).astype(jnp.float32)
    owned = returned[:, 1] + from_above + from_below
    grads = jnp.stack([query_grad, owned[0], owned[1]])
    rank_grads = jnp.einsum("jth,jrh->jtr", grads, expanded_up_weight, precision=precise_variant)
    up_terms = jnp.einsum("jtr,jth->jrh", low_full, grads, precision=precise_variant)
    down_terms = jnp.einsum("td,jtr->jdr", input_modulated, rank_grads, precision=precise_variant)
    norm_factor = 1.0 / math.sqrt(
        hidden.shape[0] * lax.axis_size("batch") * slab_rows * lax.axis_size("tiles")
    )
    grad_down, grad_up = lax.psum(
        (down_terms * norm_factor, up_terms * norm_factor), ("batch", "tiles")
    )
    return (attended.astype(jnp.bfloat16)[None], grad_down, grad_up)


def solution(mesh):
    placed = (
        P("batch", "tiles", None),
        P("batch", "tiles", None),
        P("batch", "tiles", None),
        P("batch", "tiles", None),
        P("batch", "tiles", None),
        P("batch"),
        P(),
        P(),
        P(),
        P("tiles", None),
    )
    return jax.shard_map(
        per_device,
        mesh=mesh,
        in_specs=placed,
        out_specs=(P("batch", "tiles", None), P(), P()),
        check_vma=False,
    )
```

profile of v0, /device:TPU:1, one launch (start us, length us, event | category | flops | bytes accessed | tf_op | source)
XLA Modules:
  0.0 820.5 jit_solution(3635434328755650545)
XLA Ops:
  37.3 57.5 %collective-permute-done = bf16[2,1,512,1536]{3,2,0,1:T(8,128)(2,1)} collective-permute-done((bf16[2,1,512,1536]{3,2,0,1:T(8,128)(2,1)}, bf16[2,1,512,1536]{3,2,0,1:T(8,128)(2,1)}, u32[]{:S(2)}, u32[]{:S(2)}) %collective-permute-start) | collective-permute-done | bytes 3145760 | tf_op jit(solution)/shard_map/ppermute | solution.py:21
  100.1 9.2 %pad_maximum_fusion = bf16[2,3,512,1536]{3,2,0,1:T(8,128)(2,1)} fusion(bf16[2,1,512,1536]{3,2,0,1:T(8,128)(2,1)} %collective-permute-done.1, bf16[2,1,512,1536]{3,2,0,1:T(8,128)(2,1)} %maximum_bitcast_fusion, bf16[2,1,512,1536]{3,2,0,1:T(8,128)(2,1)} %collective-permute-done), kind=kLoop, calls=%fused_computation.58 | loop fusion | flops 9437184 | bytes 18874368 | tf_op jit(solution)/shard_map/concatenate | solution.py:23
  109.3 8.6 %fusion.131 = (bf16[1,3,512,1536]{3,2,0,1:T(8,128)(2,1)}, bf16[1,3,512,1536]{3,2,0,1:T(8,128)(2,1)}) fusion(bf16[2,3,512,1536]{3,2,0,1:T(8,128)(2,1)} %pad_maximum_fusion), kind=kLoop, calls=%fused_computation.147 | loop fusion | bytes 18874368 | tf_op jit(solution)/shard_map/slice | solution.py:145
  117.9 9.1 %reshape_reshape_squeeze.6 = bf16[1536,3,4,128]{3,2,1,0:T(4,128)(2,1)} reshape(bf16[1,3,512,1536]{3,2,0,1:T(8,128)(2,1)} %get-tuple-element.142) | data formatting | bytes 9437184 | tf_op jit(solution)/shard_map/reshape;reshape;squeeze | solution.py:84
  127.0 8.5 %copy.58 = bf16[1536,3,4,128]{0,3,2,1:T(8,128)(2,1)} copy(bf16[1536,3,4,128]{3,2,1,0:T(4,128)(2,1)} %reshape_reshape_squeeze.6) | data formatting | bytes 9437184 | tf_op jit(solution)/shard_map/reshape;reshape;squeeze | solution.py:84
  135.4 9.0 %reshape_reshape_squeeze.7 = bf16[1536,3,4,128]{3,2,1,0:T(4,128)(2,1)} reshape(bf16[1,3,512,1536]{3,2,0,1:T(8,128)(2,1)} %get-tuple-element.141) | data formatting | bytes 9437184 | tf_op jit(solution)/shard_map/reshape;reshape;squeeze | solution.py:84
  149.7 327.5 %while.17 = (s32[]{:T(128)}, bf16[3,512,4,128]{1,3,2,0:T(8,128)(2,1)}, f32[3,512,4,128]{1,3,2,0:T(8,128)}, f32[3,1536,4,128]{1,3,2,0:T(8,128)}, f32[3,1536,4,128...) while((s32[]{:T(128)}, ...), condition=%wide.region_7.8_spmd.clone, body=%wide.region_3.7_spmd.clone.sunk | while | flops 4910490112 | bytes 215027920 | solution.py:89
  149.9 8.3 %fusion.167 = f32[4,512,1536]{2,1,0:T(8,128)} fusion(bf16[3,1536,4,128]{3,1,2,0:T(8,128)(2,1)} %get-tuple-element.246, s32[]{:T(128)} %get-tuple-element.228, bf16[3,512,4,128]{3,1,2,0:T(8,128)(2,1)S(1)} %get-tuple-element.245), kind=kOutput, calls=%fused_computation.25.clone.1 | convolution fusion | flops 805306368 | bytes 14681088 | tf_op jit(solution)/shard_map/while/body/eval_jaxpr/qhe,khe->hqk/dot_general | solution.py:58
  159.7 16.9 %fusion.168 = (f32[4,512]{1,0:T(4,128)S(1)}, f32[4,512,1536]{2,1,0:T(8,128)}) fusion(f32[4,512,1536]{2,1,0:T(8,128)} %fusion.167, pred[512,1536]{1,0:T(8,128)(4,1)S(1)} %copy.89), kind=kOutput, calls=%fused_computation.146.clone.1 | output fusion | flops 22021632 | bytes 25960448 | tf_op jit(solution)/shard_map/while/body/eval_jaxpr/sub | solution.py:63
  191.8 28.5 %fusion.172 = f32[3,1536,4,128]{1,3,2,0:T(8,128)} fusion(f32[3,1536,4,128]{1,3,2,0:T(8,128)} %get-tuple-element.231, s32[]{:T(128)} %get-tuple-element.228, f32[4,512,1536]{2,1,0:T(8,128)} %fusion.170, bf16[3,512,4,128]{3,1,2,0:T(8,128)(2,1)S(1)} %copy-done.6, f32[4,512,1536]{2,1,0:T(8,128)} %get-tuple-element.215, f32[4,512]{1,0:T(4,128)S(1)} %get-tuple-element.216), kind=kOutput, calls=%fused_computation.20.clone.1 | convolution fusion | flops 827330048 | bytes 54019072 | tf_op jit(solution)/shard_map/while/body/eval_jaxpr/hqk,qhe->khe/dot_general | solution.py:74
  220.3 30.5 %fusion.171 = f32[3,512,4,128]{1,3,2,0:T(8,128)} fusion(f32[3,512,4,128]{1,3,2,0:T(8,128)} %get-tuple-element.230, s32[]{:T(128)} %get-tuple-element.228, f32[4,512,1536]{2,1,0:T(8,128)} %fusion.170, bf16[3,1536,4,128]{3,1,2,0:T(8,128)(2,1)} %get-tuple-element.246, f32[4,512,1536]{2,1,0:T(8,128)} %get-tuple-element.215, ...), kind=kOutput, calls=%fused_computation.37.clone.1 | convolution fusion | flops 827330048 | bytes 52970496 | tf_op jit(solution)/shard_map/while/body/eval_jaxpr/hqk,khe->qhe/dot_general | solution.py:71
  259.0 8.3 %fusion.167 = f32[4,512,1536]{2,1,0:T(8,128)} fusion(bf16[3,1536,4,128]{3,1,2,0:T(8,128)(2,1)} %get-tuple-element.246, s32[]{:T(128)} %get-tuple-element.228, bf16[3,512,4,128]{3,1,2,0:T(8,128)(2,1)S(1)} %get-tuple-element.245), kind=kOutput, calls=%fused_computation.25.clone.1 | convolution fusion | flops 805306368 | bytes 14681088 | tf_op jit(solution)/shard_map/while/body/eval_jaxpr/qhe,khe->hqk/dot_general | solution.py:58
  268.8 16.9 %fusion.168 = (f32[4,512]{1,0:T(4,128)S(1)}, f32[4,512,1536]{2,1,0:T(8,128)}) fusion(f32[4,512,1536]{2,1,0:T(8,128)} %fusion.167, pred[512,1536]{1,0:T(8,128)(4,1)S(1)} %copy.89), kind=kOutput, calls=%fused_computation.146.clone.1 | output fusion | flops 22021632 | bytes 25960448 | tf_op jit(solution)/shard_map/while/body/eval_jaxpr/sub | solution.py:63
  300.8 28.5 %fusion.172 = f32[3,1536,4,128]{1,3,2,0:T(8,128)} fusion(f32[3,1536,4,128]{1,3,2,0:T(8,128)} %get-tuple-element.231, s32[]{:T(128)} %get-tuple-element.228, f32[4,512,1536]{2,1,0:T(8,128)} %fusion.170, bf16[3,512,4,128]{3,1,2,0:T(8,128)(2,1)S(1)} %copy-done.6, f32[4,512,1536]{2,1,0:T(8,128)} %get-tuple-element.215, f32[4,512]{1,0:T(4,128)S(1)} %get-tuple-element.216), kind=kOutput, calls=%fused_computation.20.clone.1 | convolution fusion | flops 827330048 | bytes 54019072 | tf_op jit(solution)/shard_map/while/body/eval_jaxpr/hqk,qhe->khe/dot_general | solution.py:74
  329.3 30.6 %fusion.171 = f32[3,512,4,128]{1,3,2,0:T(8,128)} fusion(f32[3,512,4,128]{1,3,2,0:T(8,128)} %get-tuple-element.230, s32[]{:T(128)} %get-tuple-element.228, f32[4,512,1536]{2,1,0:T(8,128)} %fusion.170, bf16[3,1536,4,128]{3,1,2,0:T(8,128)(2,1)} %get-tuple-element.246, f32[4,512,1536]{2,1,0:T(8,128)} %get-tuple-element.215, ...), kind=kOutput, calls=%fused_computation.37.clone.1 | convolution fusion | flops 827330048 | bytes 52970496 | tf_op jit(solution)/shard_map/while/body/eval_jaxpr/hqk,khe->qhe/dot_general | solution.py:71
  377.8 16.9 %fusion.168 = (f32[4,512]{1,0:T(4,128)S(1)}, f32[4,512,1536]{2,1,0:T(8,128)}) fusion(f32[4,512,1536]{2,1,0:T(8,128)} %fusion.167, pred[512,1536]{1,0:T(8,128)(4,1)S(1)} %copy.89), kind=kOutput, calls=%fused_computation.146.clone.1 | output fusion | flops 22021632 | bytes 25960448 | tf_op jit(solution)/shard_map/while/body/eval_jaxpr/sub | solution.py:63
  409.9 28.5 %fusion.172 = f32[3,1536,4,128]{1,3,2,0:T(8,128)} fusion(f32[3,1536,4,128]{1,3,2,0:T(8,128)} %get-tuple-element.231, s32[]{:T(128)} %get-tuple-element.228, f32[4,512,1536]{2,1,0:T(8,128)} %fusion.170, bf16[3,512,4,128]{3,1,2,0:T(8,128)(2,1)S(1)} %copy-done.6, f32[4,512,1536]{2,1,0:T(8,128)} %get-tuple-element.215, f32[4,512]{1,0:T(4,128)S(1)} %get-tuple-element.216), kind=kOutput, calls=%fused_computation.20.clone.1 | convolution fusion | flops 827330048 | bytes 54019072 | tf_op jit(solution)/shard_map/while/body/eval_jaxpr/hqk,qhe->khe/dot_general | solution.py:74
  438.4 30.5 %fusion.171 = f32[3,512,4,128]{1,3,2,0:T(8,128)} fusion(f32[3,512,4,128]{1,3,2,0:T(8,128)} %get-tuple-element.230, s32[]{:T(128)} %get-tuple-element.228, f32[4,512,1536]{2,1,0:T(8,128)} %fusion.170, bf16[3,1536,4,128]{3,1,2,0:T(8,128)(2,1)} %get-tuple-element.246, f32[4,512,1536]{2,1,0:T(8,128)} %get-tuple-element.215, ...), kind=kOutput, calls=%fused_computation.37.clone.1 | convolution fusion | flops 827330048 | bytes 52970496 | tf_op jit(solution)/shard_map/while/body/eval_jaxpr/hqk,khe->qhe/dot_general | solution.py:71
  477.3 11.9 %copy.68 = f32[1536,3,4,128]{3,2,1,0:T(4,128)} copy(f32[1536,3,4,128]{0,3,2,1:T(8,128)} %bitcast.186) | data formatting | bytes 18874368 | tf_op jit(solution)/shard_map/transpose | solution.py:87
  489.2 12.1 %stack_reshape_reshape.6 = f32[1,3,512,1536]{3,2,0,1:T(8,128)} reshape(f32[1536,3,4,128]{3,2,1,0:T(4,128)} %copy.68) | data formatting | bytes 18874368 | tf_op jit(solution)/shard_map/stack;reshape;reshape | solution.py:150
  509.4 11.9 %copy.69 = f32[1536,3,4,128]{3,2,1,0:T(4,128)} copy(f32[1536,3,4,128]{0,3,2,1:T(8,128)} %bitcast.187) | data formatting | bytes 18874368 | tf_op jit(solution)/shard_map/transpose | solution.py:87
  521.3 12.1 %stack_reshape_reshape.7 = f32[1,3,512,1536]{3,2,0,1:T(8,128)} reshape(f32[1536,3,4,128]{3,2,1,0:T(4,128)} %copy.69) | data formatting | bytes 18874368 | tf_op jit(solution)/shard_map/stack;reshape;reshape | solution.py:150
  562.5 59.3 %collective-permute-done.2 = bf16[2,512,1536]{2,1,0:T(8,128)(2,1)} collective-permute-done((bf16[2,512,1536]{2,1,0:T(8,128)(2,1)}, bf16[2,512,1536]{2,1,0:T(8,128)(2,1)}, u32[]{:S(2)}, u32[]{:S(2)}) %collective-permute-start.2) | collective-permute-done | bytes 3145760 | tf_op jit(solution)/shard_map/ppermute | solution.py:30
  645.2 163.8 %all-reduce.3.cloned.1.call-done = (f32[3,3072,32]{1,2,0:T(8,128)}, f32[3,32,1536]{2,1,0:T(8,128)}) async-done(((f32[3,3072,32]{1,2,0:T(8,128)}, f32[3,32,1536]{2,1,0:T(8,128)}), (f32[3,3072,32]{1,2,0:T(8,128)}, f32[3,32,1536]{2,1,0:T(8,128)})) %all-reduce.3.cloned.1.call-update) | async-done | bytes 1769488 | tf_op jit(solution)/shard_map/psum | solution.py:163
  (126 shorter events, 187.3 us)
Async XLA Ops:
  7.2 6.2 copy-start
  7.2 7.1 copy-start.22
  7.2 801.8 %all-reduce.3.cloned.1.call-start = ((), (), s32[]{:S(2)}) async-start(), calls=%async_computation | async-start | bytes 3538944 | tf_op jit(solution)/shard_map/psum | solution.py:163
  7.2 7.0 copy-start.3
  9.8 6.0 copy-start.17
  21.6 9.2 %copy-start.19 = (s32[4,27]{1,0:T(4,128)S(1)}, s32[4,27]{1,0:T(4,128)}, u32[]{:S(2)}) copy-start(s32[4,27]{1,0:T(4,128)} %param.21) | copy-start | bytes 1300
  23.6 71.1 %collective-permute-start = (bf16[2,1,512,1536]{3,2,0,1:T(8,128)(2,1)}, bf16[2,1,512,1536]{3,2,0,1:T(8,128)(2,1)}, u32[]{:S(2)}, u32[]{:S(2)}) collective-permute-start(bf16[2,1,512,1536]{3,2,0,1:T(8,128)(2,1)} %maximum_bitcast_fusion), channel_id=1, source_target_pairs={{0,1},{1,2},{2,3},{3,4},{4,5},{5,6},{6,7},{7,8},{8,9},{9,10},{10,1... | collective-permute-start | bytes 9437192 | tf_op jit(solution)/shard_map/ppermute | solution.py:21
  29.3 70.8 %collective-permute-start.1 = (bf16[2,1,512,1536]{3,2,0,1:T(8,128)(2,1)}, bf16[2,1,512,1536]{3,2,0,1:T(8,128)(2,1)}, u32[]{:S(2)}, u32[]{:S(2)}) collective-permute-start(bf16[2,1,512,1536]{3,2,0,1:T(8,128)(2,1)} %maximum_bitcast_fusion), channel_id=1, source_target_pairs={{1,0},{2,1},{3,2},{4,3},{5,4},{6,5},{7,6},{8,7},{9,8},{10,9},{11,1... | collective-permute-start | bytes 9437192 | tf_op jit(solution)/shard_map/ppermute | solution.py:22
  149.9 8.3 %copy-start.5 = (bf16[3,512,4,128]{3,1,2,0:T(8,128)(2,1)}, bf16[3,512,4,128]{3,1,2,0:T(8,128)(2,1)S(1)}, u32[]{:S(2)}) copy-start(bf16[3,512,4,128]{3,1,2,0:T(8,128)(2,1)S(1)} %get-tuple-element.245) | copy-start | bytes 4718596 | tf_op jit(solution)/shard_map/while
  159.7 16.9 %copy-start.7 = (bf16[3,512,4,128]{1,3,2,0:T(8,128)(2,1)S(1)}, bf16[3,512,4,128]{1,3,2,0:T(8,128)(2,1)}, u32[]{:S(2)}) copy-start(bf16[3,512,4,128]{1,3,2,0:T(8,128)(2,1)} %get-tuple-element.247) | copy-start | bytes 4718596 | tf_op jit(solution)/shard_map/while
  184.0 7.8 copy-start.6
  259.0 8.3 %copy-start.5 = (bf16[3,512,4,128]{3,1,2,0:T(8,128)(2,1)}, bf16[3,512,4,128]{3,1,2,0:T(8,128)(2,1)S(1)}, u32[]{:S(2)}) copy-start(bf16[3,512,4,128]{3,1,2,0:T(8,128)(2,1)S(1)} %get-tuple-element.245) | copy-start | bytes 4718596 | tf_op jit(solution)/shard_map/while
  268.8 16.9 %copy-start.7 = (bf16[3,512,4,128]{1,3,2,0:T(8,128)(2,1)S(1)}, bf16[3,512,4,128]{1,3,2,0:T(8,128)(2,1)}, u32[]{:S(2)}) copy-start(bf16[3,512,4,128]{1,3,2,0:T(8,128)(2,1)} %get-tuple-element.247) | copy-start | bytes 4718596 | tf_op jit(solution)/shard_map/while
  293.0 7.8 copy-start.6
  368.0 8.3 %copy-start.5 = (bf16[3,512,4,128]{3,1,2,0:T(8,128)(2,1)}, bf16[3,512,4,128]{3,1,2,0:T(8,128)(2,1)S(1)}, u32[]{:S(2)}) copy-start(bf16[3,512,4,128]{3,1,2,0:T(8,128)(2,1)S(1)} %get-tuple-element.245) | copy-start | bytes 4718596 | tf_op jit(solution)/shard_map/while
  377.8 16.9 %copy-start.7 = (bf16[3,512,4,128]{1,3,2,0:T(8,128)(2,1)S(1)}, bf16[3,512,4,128]{1,3,2,0:T(8,128)(2,1)}, u32[]{:S(2)}) copy-start(bf16[3,512,4,128]{1,3,2,0:T(8,128)(2,1)} %get-tuple-element.247) | copy-start | bytes 4718596 | tf_op jit(solution)/shard_map/while
  402.0 7.8 copy-start.6
  552.0 69.9 %collective-permute-start.2 = (bf16[2,512,1536]{2,1,0:T(8,128)(2,1)}, bf16[2,512,1536]{2,1,0:T(8,128)(2,1)}, u32[]{:S(2)}, u32[]{:S(2)}) collective-permute-start(bf16[2,512,1536]{2,1,0:T(8,128)(2,1)} %get-tuple-element.139), channel_id=1, source_target_pairs={{1,0},{2,1},{3,2},{4,3},{5,4},{6,5},{7,6},{8,7},{9,8},{10,9},{11,1... | collective-permute-start | bytes 9437192 | tf_op jit(solution)/shard_map/ppermute | solution.py:30
  553.3 69.5 %collective-permute-start.3 = (bf16[2,512,1536]{2,1,0:T(8,128)(2,1)}, bf16[2,512,1536]{2,1,0:T(8,128)(2,1)}, u32[]{:S(2)}, u32[]{:S(2)}) collective-permute-start(bf16[2,512,1536]{2,1,0:T(8,128)(2,1)} %get-tuple-element.140), channel_id=1, source_target_pairs={{0,1},{1,2},{2,3},{3,4},{4,5},{5,6},{6,7},{7,8},{8,9},{9,10},{10,1... | collective-permute-start | bytes 9437192 | tf_op jit(solution)/shard_map/ppermute | solution.py:30
  562.5 66.1 %copy-start.2 = (f32[1,512,1536]{2,1,0:T(8,128)S(1)}, f32[1,512,1536]{2,1,0:T(8,128)}, u32[]{:S(2)}) copy-start(f32[1,512,1536]{2,1,0:T(8,128)} %copy.77) | copy-start | bytes 9437188
  562.5 66.1 %copy-start.12 = (f32[512,96]{0,1:S(1)}, f32[512,96]{0,1}, u32[]{:S(2)}) copy-start(f32[512,96]{0,1} %copy-done.11) | copy-start | bytes 589828
  633.0 4.7 copy-start.18
  637.8 5.8 copy-start.10
  637.8 175.5 %copy-start.1 = (f32[50,2,3072]{2,1,0:T(2,128)S(1)}, f32[50,2,3072]{2,1,0:T(2,128)}, u32[]{:S(2)}) copy-start(f32[50,2,3072]{2,1,0:T(2,128)} %param.18) | copy-start | bytes 3686404
  (10 other events, 32.5 us)
Sparse Core Ops, SparseCore 0:
  643.7 165.1 all-reduce.2
where the time goes:
time: 831 us; the launch traced here: 820 us
  matrix products  290 us (35%)
  waiting for transfers between devices  287 us (35%)
  local copies, waits for them, and re-layouts  128 us (15%)
  other arithmetic  85.4 us (10%)
  between operations  15.5 us (2%)
  starting transfers between devices  13.9 us (2%)
    psum x1, waiting for transfers between devices, per_device(): lax.psum((down_terms * norm_factor, up_terms * norm_factor), ('batch', 't...  164 us
    dot_general x3, matrix products, attend_group(): jnp.einsum('hqk,khe->qhe', score_grad, key_rows, preferred_element_type=j...  91.6 us
    dot_general x3, matrix products, attend_group(): jnp.einsum('hqk,qhe->khe', score_grad, queries, preferred_element_type=jn...  85.5 us
    ppermute x2, waiting for transfers between devices, shifted(): lax.ppermute(value, axis, [(source, source + steps) for source in range(i...  60.2 us
    ppermute x1, waiting for transfers between devices, extended(): before = lax.ppermute(last, axis, up)  57.5 us
    sub x3, other arithmetic, attend_group(): weights = jnp.where(allowed[None], jnp.exp(scores - row_max), 0.0)  50.7 us
    another operation x3, local copies, waits for them, and re-layouts, per_device(): jnp.stack([key_grad.reshape(3, slab_rows, across), value_grad.reshape(3,...  32.3 us
    another operation x4, local copies, waits for them, and re-layouts, split_heads(): tensor.reshape(tensor.shape[0], groups, 4, HEAD).transpose(1, 0, 2, 3)  31.8 us
  transfers between devices with their start and end apart: 5, of which 5 were waited for; matrix products, arithmetic and copies ran while one was open for 1% of the time, Pallas kernels for 0%

commit v1 on v0

--- a/solution.py
+++ b/solution.py
@@ -161,7 +161,7 @@
         hidden.shape[0] * lax.axis_size("batch") * slab_rows * lax.axis_size("tiles")
     )
     grad_down, grad_up = lax.psum(
-        (down_terms * norm_factor, up_terms * norm_factor), ("batch", "tiles")
+        lax.psum((down_terms * norm_factor, up_terms * norm_factor), "batch"), "tiles"
     )
     return (attended.astype(jnp.bfloat16)[None], grad_down, grad_up)
 

time: 831 us -> 1090 us (1.31)
  the two profiles are of different devices: /device:TPU:1 before, /device:TPU:0 now
where the time goes in v1:
time: 1090 us; the launch traced here: 1080 us
  waiting for transfers between devices  548 us (50%)
  matrix products  291 us (27%)
  local copies, waits for them, and re-layouts  128 us (12%)
  other arithmetic  85.3 us (8%)
  between operations  15.5 us (1%)
  starting transfers between devices  14.1 us (1%)
    psum x1, waiting for transfers between devices, per_device(): lax.psum(lax.psum((down_terms * norm_factor, up_terms * norm_factor), 'ba...  358 us
    dot_general x3, matrix products, attend_group(): jnp.einsum('hqk,khe->qhe', score_grad, key_rows, preferred_element_type=j...  91.7 us
    dot_general x3, matrix products, attend_group(): jnp.einsum('hqk,qhe->khe', score_grad, queries, preferred_element_type=jn...  85.4 us
    psum x1, waiting for transfers between devices, per_device(): lax.psum((down_terms * norm_factor, up_terms * norm_factor), 'batch')  65.1 us
    ppermute x2, waiting for transfers between devices, shifted(): lax.ppermute(value, axis, [(source, source + steps) for source in range(i...  60.9 us
    ppermute x1, waiting for transfers between devices, extended(): before = lax.ppermute(last, axis, up)  58.1 us
    sub x3, other arithmetic, attend_group(): weights = jnp.where(allowed[None], jnp.exp(scores - row_max), 0.0)  50.5 us
    another operation x3, local copies, waits for them, and re-layouts, per_device(): jnp.stack([key_grad.reshape(3, slab_rows, across), value_grad.reshape(3,...  32.3 us
  transfers between devices with their start and end apart: 6, of which 6 were waited for; matrix products, arithmetic and copies ran while one was open for 1% of the time, Pallas kernels for 0%

profile of v1, /device:TPU:0, one launch (start us, length us, event | category | flops | bytes accessed | tf_op | source)
XLA Modules:
  0.0 1081.6 jit_solution(4000470437627234636)
XLA Ops:
  36.8 58.1 %collective-permute-done = bf16[2,1,512,1536]{3,2,0,1:T(8,128)(2,1)} collective-permute-done((bf16[2,1,512,1536]{3,2,0,1:T(8,128)(2,1)}, bf16[2,1,512,1536]{3,2,0,1:T(8,128)(2,1)}, u32[]{:S(2)}, u32[]{:S(2)}) %collective-permute-start) | collective-permute-done | bytes 3145760 | tf_op jit(solution)/shard_map/ppermute | solution.py:21
  100.6 9.2 pad_maximum_fusion
  109.8 8.6 fusion.131
  118.4 9.0 reshape_reshape_squeeze.6
  127.5 8.4 copy.58
  135.9 9.0 reshape_reshape_squeeze.7
  150.2 327.4 %while.17 = (s32[]{:T(128)}, bf16[3,512,4,128]{1,3,2,0:T(8,128)(2,1)}, f32[3,512,4,128]{1,3,2,0:T(8,128)}, f32[3,1536,4,128]{1,3,2,0:T(8,128)}, f32[3,1536,4,128...) while((s32[]{:T(128)}, ...), condition=%wide.region_7.8_spmd.clone, body=%wide.region_3.7_spmd.clone.sunk | while | flops 4910490112 | bytes 215027920 | solution.py:89
  150.3 8.3 fusion.167
  160.1 16.8 %fusion.168 = (f32[4,512]{1,0:T(4,128)S(1)}, f32[4,512,1536]{2,1,0:T(8,128)}) fusion(f32[4,512,1536]{2,1,0:T(8,128)} %fusion.167, pred[512,1536]{1,0:T(8,128)(4,1)S(1)} %copy.89), kind=kOutput, calls=%fused_computation.146.clone.1 | output fusion | flops 22021632 | bytes 25960448 | tf_op jit(solution)/shard_map/while/body/eval_jaxpr/sub | solution.py:63
  192.3 28.5 %fusion.172 = f32[3,1536,4,128]{1,3,2,0:T(8,128)} fusion(f32[3,1536,4,128]{1,3,2,0:T(8,128)} %get-tuple-element.233, s32[]{:T(128)} %get-tuple-element.230, f32[4,512,1536]{2,1,0:T(8,128)} %fusion.170, bf16[3,512,4,128]{3,1,2,0:T(8,128)(2,1)S(1)} %copy-done.6, f32[4,512,1536]{2,1,0:T(8,128)} %get-tuple-element.217, f32[4,512]{1,0:T(4,128)S(1)} %get-tuple-element.218), kind=kOutput, calls=%fused_computation.20.clone.1 | convolution fusion | flops 827330048 | bytes 54019072 | tf_op jit(solution)/shard_map/while/body/eval_jaxpr/hqk,qhe->khe/dot_general | solution.py:74
  220.7 30.5 %fusion.171 = f32[3,512,4,128]{1,3,2,0:T(8,128)} fusion(f32[3,512,4,128]{1,3,2,0:T(8,128)} %get-tuple-element.232, s32[]{:T(128)} %get-tuple-element.230, f32[4,512,1536]{2,1,0:T(8,128)} %fusion.170, bf16[3,1536,4,128]{3,1,2,0:T(8,128)(2,1)} %get-tuple-element.248, f32[4,512,1536]{2,1,0:T(8,128)} %get-tuple-element.217, ...), kind=kOutput, calls=%fused_computation.37.clone.1 | convolution fusion | flops 827330048 | bytes 52970496 | tf_op jit(solution)/shard_map/while/body/eval_jaxpr/hqk,khe->qhe/dot_general | solution.py:71
  269.2 16.8 %fusion.168 = (f32[4,512]{1,0:T(4,128)S(1)}, f32[4,512,1536]{2,1,0:T(8,128)}) fusion(f32[4,512,1536]{2,1,0:T(8,128)} %fusion.167, pred[512,1536]{1,0:T(8,128)(4,1)S(1)} %copy.89), kind=kOutput, calls=%fused_computation.146.clone.1 | output fusion | flops 22021632 | bytes 25960448 | tf_op jit(solution)/shard_map/while/body/eval_jaxpr/sub | solution.py:63
  301.2 28.5 %fusion.172 = f32[3,1536,4,128]{1,3,2,0:T(8,128)} fusion(f32[3,1536,4,128]{1,3,2,0:T(8,128)} %get-tuple-element.233, s32[]{:T(128)} %get-tuple-element.230, f32[4,512,1536]{2,1,0:T(8,128)} %fusion.170, bf16[3,512,4,128]{3,1,2,0:T(8,128)(2,1)S(1)} %copy-done.6, f32[4,512,1536]{2,1,0:T(8,128)} %get-tuple-element.217, f32[4,512]{1,0:T(4,128)S(1)} %get-tuple-element.218), kind=kOutput, calls=%fused_computation.20.clone.1 | convolution fusion | flops 827330048 | bytes 54019072 | tf_op jit(solution)/shard_map/while/body/eval_jaxpr/hqk,qhe->khe/dot_general | solution.py:74
  329.6 30.6 %fusion.171 = f32[3,512,4,128]{1,3,2,0:T(8,128)} fusion(f32[3,512,4,128]{1,3,2,0:T(8,128)} %get-tuple-element.232, s32[]{:T(128)} %get-tuple-element.230, f32[4,512,1536]{2,1,0:T(8,128)} %fusion.170, bf16[3,1536,4,128]{3,1,2,0:T(8,128)(2,1)} %get-tuple-element.248, f32[4,512,1536]{2,1,0:T(8,128)} %get-tuple-element.217, ...), kind=kOutput, calls=%fused_computation.37.clone.1 | convolution fusion | flops 827330048 | bytes 52970496 | tf_op jit(solution)/shard_map/while/body/eval_jaxpr/hqk,khe->qhe/dot_general | solution.py:71
  378.2 16.8 %fusion.168 = (f32[4,512]{1,0:T(4,128)S(1)}, f32[4,512,1536]{2,1,0:T(8,128)}) fusion(f32[4,512,1536]{2,1,0:T(8,128)} %fusion.167, pred[512,1536]{1,0:T(8,128)(4,1)S(1)} %copy.89), kind=kOutput, calls=%fused_computation.146.clone.1 | output fusion | flops 22021632 | bytes 25960448 | tf_op jit(solution)/shard_map/while/body/eval_jaxpr/sub | solution.py:63
  410.3 28.5 %fusion.172 = f32[3,1536,4,128]{1,3,2,0:T(8,128)} fusion(f32[3,1536,4,128]{1,3,2,0:T(8,128)} %get-tuple-element.233, s32[]{:T(128)} %get-tuple-element.230, f32[4,512,1536]{2,1,0:T(8,128)} %fusion.170, bf16[3,512,4,128]{3,1,2,0:T(8,128)(2,1)S(1)} %copy-done.6, f32[4,512,1536]{2,1,0:T(8,128)} %get-tuple-element.217, f32[4,512]{1,0:T(4,128)S(1)} %get-tuple-element.218), kind=kOutput, calls=%fused_computation.20.clone.1 | convolution fusion | flops 827330048 | bytes 54019072 | tf_op jit(solution)/shard_map/while/body/eval_jaxpr/hqk,qhe->khe/dot_general | solution.py:74
  438.7 30.5 %fusion.171 = f32[3,512,4,128]{1,3,2,0:T(8,128)} fusion(f32[3,512,4,128]{1,3,2,0:T(8,128)} %get-tuple-element.232, s32[]{:T(128)} %get-tuple-element.230, f32[4,512,1536]{2,1,0:T(8,128)} %fusion.170, bf16[3,1536,4,128]{3,1,2,0:T(8,128)(2,1)} %get-tuple-element.248, f32[4,512,1536]{2,1,0:T(8,128)} %get-tuple-element.217, ...), kind=kOutput, calls=%fused_computation.37.clone.1 | convolution fusion | flops 827330048 | bytes 52970496 | tf_op jit(solution)/shard_map/while/body/eval_jaxpr/hqk,khe->qhe/dot_general | solution.py:71
  477.6 11.9 %copy.68 = f32[1536,3,4,128]{3,2,1,0:T(4,128)} copy(f32[1536,3,4,128]{0,3,2,1:T(8,128)} %bitcast.186) | data formatting | bytes 18874368 | tf_op jit(solution)/shard_map/transpose | solution.py:87
  489.5 12.0 %stack_reshape_reshape.6 = f32[1,3,512,1536]{3,2,0,1:T(8,128)} reshape(f32[1536,3,4,128]{3,2,1,0:T(4,128)} %copy.68) | data formatting | bytes 18874368 | tf_op jit(solution)/shard_map/stack;reshape;reshape | solution.py:150
  509.7 11.9 %copy.69 = f32[1536,3,4,128]{3,2,1,0:T(4,128)} copy(f32[1536,3,4,128]{0,3,2,1:T(8,128)} %bitcast.187) | data formatting | bytes 18874368 | tf_op jit(solution)/shard_map/transpose | solution.py:87
  521.6 12.0 %stack_reshape_reshape.7 = f32[1,3,512,1536]{3,2,0,1:T(8,128)} reshape(f32[1536,3,4,128]{3,2,1,0:T(4,128)} %copy.69) | data formatting | bytes 18874368 | tf_op jit(solution)/shard_map/stack;reshape;reshape | solution.py:150
  563.4 59.7 %collective-permute-done.2 = bf16[2,512,1536]{2,1,0:T(8,128)(2,1)} collective-permute-done((bf16[2,512,1536]{2,1,0:T(8,128)(2,1)}, bf16[2,512,1536]{2,1,0:T(8,128)(2,1)}, u32[]{:S(2)}, u32[]{:S(2)}) %collective-permute-start.2) | collective-permute-done | bytes 3145760 | tf_op jit(solution)/shard_map/ppermute | solution.py:30
  645.2 65.1 %all-reduce.7.cloned.1.call-done = (f32[3,3072,32]{1,2,0:T(8,128)}, f32[3,32,1536]{2,1,0:T(8,128)}) async-done(((f32[3,3072,32]{1,2,0:T(8,128)}, f32[3,32,1536]{2,1,0:T(8,128)}), (f32[3,3072,32]{1,2,0:T(8,128)}, f32[3,32,1536]{2,1,0:T(8,128)})) %all-reduce.7.cloned.1.call-update) | async-done | bytes 1769488 | tf_op jit(solution)/shard_map/psum | solution.py:164
  711.9 358.2 %all-reduce.5.cloned.1.call-done = (f32[3,3072,32]{1,2,0:T(8,128)}, f32[3,32,1536]{2,1,0:T(8,128)}) async-done(((f32[3,3072,32]{1,2,0:T(8,128)}, f32[3,32,1536]{2,1,0:T(8,128)}), (f32[3,3072,32]{1,2,0:T(8,128)}, f32[3,32,1536]{2,1,0:T(8,128)})) %all-reduce.5.cloned.1.call-update) | async-done | bytes 1769488 | tf_op jit(solution)/shard_map/psum | solution.py:163
  (129 shorter events, 196.4 us)
Async XLA Ops:
  7.2 6.2 copy-start
  7.2 7.1 copy-start.22
  7.2 703.1 %all-reduce.7.cloned.1.call-start = ((), (), s32[]{:S(2)}) async-start(), calls=%async_computation.1 | async-start | bytes 3538944 | tf_op jit(solution)/shard_map/psum | solution.py:164
  7.2 7.0 copy-start.3
  9.8 6.0 copy-start.17
  21.6 8.8 copy-start.19
  23.6 71.2 %collective-permute-start = (bf16[2,1,512,1536]{3,2,0,1:T(8,128)(2,1)}, bf16[2,1,512,1536]{3,2,0,1:T(8,128)(2,1)}, u32[]{:S(2)}, u32[]{:S(2)}) collective-permute-start(bf16[2,1,512,1536]{3,2,0,1:T(8,128)(2,1)} %maximum_bitcast_fusion), channel_id=1, source_target_pairs={{0,1},{1,2},{2,3},{3,4},{4,5},{5,6},{6,7},{7,8},{8,9},{9,10},{10,1... | collective-permute-start | bytes 9437192 | tf_op jit(solution)/shard_map/ppermute | solution.py:21
  28.8 71.8 %collective-permute-start.1 = (bf16[2,1,512,1536]{3,2,0,1:T(8,128)(2,1)}, bf16[2,1,512,1536]{3,2,0,1:T(8,128)(2,1)}, u32[]{:S(2)}, u32[]{:S(2)}) collective-permute-start(bf16[2,1,512,1536]{3,2,0,1:T(8,128)(2,1)} %maximum_bitcast_fusion), channel_id=1, source_target_pairs={{1,0},{2,1},{3,2},{4,3},{5,4},{6,5},{7,6},{8,7},{9,8},{10,9},{11,1... | collective-permute-start | bytes 9437192 | tf_op jit(solution)/shard_map/ppermute | solution.py:22
  150.3 8.3 copy-start.5
  160.1 16.8 %copy-start.7 = (bf16[3,512,4,128]{1,3,2,0:T(8,128)(2,1)S(1)}, bf16[3,512,4,128]{1,3,2,0:T(8,128)(2,1)}, u32[]{:S(2)}) copy-start(bf16[3,512,4,128]{1,3,2,0:T(8,128)(2,1)} %get-tuple-element.249) | copy-start | bytes 4718596 | tf_op jit(solution)/shard_map/while
  184.4 7.9 copy-start.6
  259.4 8.3 copy-start.5
  269.2 16.8 %copy-start.7 = (bf16[3,512,4,128]{1,3,2,0:T(8,128)(2,1)S(1)}, bf16[3,512,4,128]{1,3,2,0:T(8,128)(2,1)}, u32[]{:S(2)}) copy-start(bf16[3,512,4,128]{1,3,2,0:T(8,128)(2,1)} %get-tuple-element.249) | copy-start | bytes 4718596 | tf_op jit(solution)/shard_map/while
  293.3 7.9 copy-start.6
  368.4 8.3 copy-start.5
  378.2 16.8 %copy-start.7 = (bf16[3,512,4,128]{1,3,2,0:T(8,128)(2,1)S(1)}, bf16[3,512,4,128]{1,3,2,0:T(8,128)(2,1)}, u32[]{:S(2)}) copy-start(bf16[3,512,4,128]{1,3,2,0:T(8,128)(2,1)} %get-tuple-element.249) | copy-start | bytes 4718596 | tf_op jit(solution)/shard_map/while
  402.4 7.9 copy-start.6
  552.3 70.8 %collective-permute-start.2 = (bf16[2,512,1536]{2,1,0:T(8,128)(2,1)}, bf16[2,512,1536]{2,1,0:T(8,128)(2,1)}, u32[]{:S(2)}, u32[]{:S(2)}) collective-permute-start(bf16[2,512,1536]{2,1,0:T(8,128)(2,1)} %get-tuple-element.141), channel_id=1, source_target_pairs={{1,0},{2,1},{3,2},{4,3},{5,4},{6,5},{7,6},{8,7},{9,8},{10,9},{11,1... | collective-permute-start | bytes 9437192 | tf_op jit(solution)/shard_map/ppermute | solution.py:30
  553.6 70.7 %collective-permute-start.3 = (bf16[2,512,1536]{2,1,0:T(8,128)(2,1)}, bf16[2,512,1536]{2,1,0:T(8,128)(2,1)}, u32[]{:S(2)}, u32[]{:S(2)}) collective-permute-start(bf16[2,512,1536]{2,1,0:T(8,128)(2,1)} %get-tuple-element.142), channel_id=1, source_target_pairs={{0,1},{1,2},{2,3},{3,4},{4,5},{5,6},{6,7},{7,8},{8,9},{9,10},{10,1... | collective-permute-start | bytes 9437192 | tf_op jit(solution)/shard_map/ppermute | solution.py:30
  563.4 66.8 %copy-start.2 = (f32[1,512,1536]{2,1,0:T(8,128)S(1)}, f32[1,512,1536]{2,1,0:T(8,128)}, u32[]{:S(2)}) copy-start(f32[1,512,1536]{2,1,0:T(8,128)} %copy.77) | copy-start | bytes 9437188
  563.4 66.8 %copy-start.12 = (f32[512,96]{0,1:S(1)}, f32[512,96]{0,1}, u32[]{:S(2)}) copy-start(f32[512,96]{0,1} %copy-done.11) | copy-start | bytes 589828
  639.3 71.0 %copy-start.10 = (bf16[3,512,4,128]{1,3,2,0:T(8,128)(2,1)S(1)}, bf16[3,512,4,128]{1,3,2,0:T(8,128)(2,1)}, u32[]{:S(2)}) copy-start(bf16[3,512,4,128]{1,3,2,0:T(8,128)(2,1)} %get-tuple-element.58) | copy-start | bytes 4718596
  639.3 435.1 %copy-start.1 = (f32[50,2,3072]{2,1,0:T(2,128)S(1)}, f32[50,2,3072]{2,1,0:T(2,128)}, u32[]{:S(2)}) copy-start(f32[50,2,3072]{2,1,0:T(2,128)} %param.18) | copy-start | bytes 3686404
  645.1 425.0 %all-reduce.5.cloned.1.call-start = ((), (), s32[]{:S(2)}) async-start(), calls=%async_computation | async-start | bytes 3538944 | tf_op jit(solution)/shard_map/psum | solution.py:163
  (11 other events, 37.2 us)
Sparse Core Ops, SparseCore 0:
  645.2 64.9 all-reduce.6
  713.0 357.0 all-reduce.4
